TPU v7x, 32 devices: a whole 2x2x4 slice. The times are simulated.
32 devices in a mesh: dp: 4 (over y, core), mp: 8 (over z, x).
Axes of the slice: x: 2, y: 2, z: 4, core: 2. Of those that a mesh axis runs over, the one named last changes fastest.
Arguments:
- query_rows: bfloat16 [8192, 16, 128], P('dp', 'mp'), may hold values from -8 to 8
- key_rows: bfloat16 [8192, 16, 128], P('dp', 'mp'), may hold values from -8 to 8
- value_rows: bfloat16 [8192, 16, 128], P('dp', 'mp'), may hold values from -6 to 6
- residual: bfloat16 [4096, 8, 768], P('dp', 'mp'), may hold values from -40 to 40
- lengths: int32 [64], replicated, may hold values from 1 to 256, as said below
- assignment: int32 [64], replicated, may hold values from 0 to 3, as said below
- out_proj: bfloat16 [1024, 1536], P(None, 'mp'), may hold values from -0.1875 to 0.1875
- norm_gain: float32 [1536], replicated, may hold values from 0.5 to 1.5
- norm_bias: float32 [1536], replicated, may hold values from -3 to 3
- glu_proj: bfloat16 [1536, 3072], P(None, 'mp'), may hold values from -0.15625 to 0.15625
- conv_taps: float32 [31, 1536], replicated, may hold values from -1 to 1
- batch_scale: float32 [1536], replicated, may hold values from 0.25 to 1.75
- batch_shift: float32 [1536], replicated, may hold values from -3 to 3
- down_proj: bfloat16 [1536, 1536], P(None, 'mp'), may hold values from -0.15625 to 0.15625
Outputs:
- encoded: bfloat16 [16384, 1536], P(('dp', 'mp'))
Inputs may be any that keep to these rules, and one draw needn't show every extreme that they name: `lengths`: utterance u starts in data group u // 16; a data group holds its utterances in order of u from its first frame on, and its frames after them are padding. In every draw every data group sends exactly 256 frames in each of its 4 utterances to one and the same data group, so that this group receives 4 * 256 frames from every data group; the utterances one data group sends to one data group never have more frames together. `assignment`: every data group sends exactly 4 of its utterances to each data group, itself included. In its new group an utterance lies after those of lower number, from the first frame on, and the frames after them are padding.
All inputs are finite; a program needn't handle non-finite values.
Results may differ from a plain program's by a relative error of at most 0.0034.
Values may be sent and summed in bfloat16 or wider, within the bound.
A program may use at most 128 MiB of HBM per device.

v0:
```python
import jax
import jax.numpy as jnp
from jax import lax
from jax.sharding import PartitionSpec as P

HD = 64
KERNEL = 31
HALF = 15
MAXLEN = 256
PIECES = 4
QBLK = 512
EPS = 1e-05
MASKED = -1e30


def with_halo(cells, sides, width):
    for axis, dim in sides:
        count = lax.axis_size(axis)
        ends = count - 1
        head = lax.slice_in_dim(cells, 0, width, axis=dim)
        tail = lax.slice_in_dim(cells, cells.shape[dim] - width, cells.shape[dim], axis=dim)
        cells = jnp.concatenate(
            [
                lax.ppermute(tail, axis, [(i, (i + 1) % count) for i in range(ends)]),
                cells,
                lax.ppermute(head, axis, [((i + 1) % count, i) for i in range(ends)]),
            ],
            axis=dim,
        )
    return cells


def unpack_pairs(packed):
    pair_rows, head_count, pair_width = packed.shape
    width = pair_width // 2
    return (
        packed.reshape(pair_rows, head_count, 2, width)
        .transpose(0, 2, 1, 3)
        .reshape(pair_rows * 2, head_count * width)
    )


def unpack_fours(packed):
    four_rows, block_count, four_width = packed.shape
    width = four_width // 4
    return (
        packed.reshape(four_rows, block_count, 4, width)
        .transpose(0, 2, 1, 3)
        .reshape(four_rows * 4, block_count * width)
    )


def utterance_tables(lengths, assignment, per_group):
    utterance_count = lengths.shape[0]
    utterance = jnp.arange(utterance_count, dtype=jnp.int32)
    source = utterance // per_group
    earlier = utterance[None, :] < utterance[:, None]
    same_source = source[None, :] == source[:, None]
    same_target = assignment[None, :] == assignment[:, None]
    span_table = jnp.broadcast_to(lengths[None, :], (utterance_count, utterance_count))
    nothing = jnp.zeros_like(span_table)
    before_start = jnp.sum(jnp.where(earlier & same_source, span_table, nothing), axis=1)
    after_start = jnp.sum(jnp.where(earlier & same_target, span_table, nothing), axis=1)
    slot_first = jnp.sum(
        jnp.where(earlier & same_source & same_target, span_table, nothing), axis=1
    )
    return (source, before_start, after_start, slot_first)


def find_frames(data_group, owner_group, first_frame, lengths, frames, lookup):
    position = jnp.arange(frames, dtype=jnp.int32)[:, None]
    matches = (
        (owner_group[None, :] == data_group)
        & (position >= first_frame[None, :])
        & (position < first_frame[None, :] + lengths[None, :])
    )
    utterance = jnp.arange(lengths.shape[0], dtype=jnp.int32)[None, :]
    occupied_slots = jnp.any(matches, axis=1)
    segment = jnp.where(occupied_slots, jnp.sum(jnp.where(matches, utterance, 0), axis=1), -1)
    shifted = jnp.sum(jnp.where(matches, lookup[None, :] - first_frame[None, :], 0), axis=1)
    source_row = jnp.where(occupied_slots, jnp.arange(frames, dtype=jnp.int32) + shifted, 0)
    return (segment, occupied_slots, source_row)


def outgoing_rows(
    data_group, groups, per_group, capacity, lengths, assignment, before_start, slot_first
):
    first_id = data_group * per_group
    own_length = lax.dynamic_slice_in_dim(lengths, first_id, per_group)
    own_target = lax.dynamic_slice_in_dim(assignment, first_id, per_group)
    own_before = lax.dynamic_slice_in_dim(before_start, first_id, per_group)
    own_slot = lax.dynamic_slice_in_dim(slot_first, first_id, per_group)
    slot_index = jnp.arange(groups * capacity, dtype=jnp.int32)
    target = (slot_index // capacity)[:, None]
    slot_place = (slot_index % capacity)[:, None]
    matches = (
        (own_target[None, :] == target)
        & (slot_place >= own_slot[None, :])
        & (slot_place < own_slot[None, :] + own_length[None, :])
    )
    valid_slot = jnp.any(matches, axis=1)
    send_frame = jnp.sum(
        jnp.where(matches, own_before[None, :] - own_slot[None, :] + slot_place, 0), axis=1
    )
    return (send_frame, valid_slot)


def pack_outgoing(stacked, send_frame, valid_slot):
    picked = jnp.take(stacked, send_frame, axis=0)
    return jnp.where(valid_slot[:, None], picked, jnp.zeros((), stacked.dtype))


def finalize_rows(received_rows, occupied_slots, incoming_row):
    picked = jnp.take(received_rows, incoming_row, axis=0)
    return jnp.where(occupied_slots[:, None], picked, jnp.zeros((), received_rows.dtype))


def attend(query_rows, key_rows, value_rows, segment, live_count):
    group_rows, width_per_head = query_rows.shape
    head_count = width_per_head // HD
    window = QBLK + 2 * MAXLEN
    score_scale = HD ** (-0.5)
    queries = query_rows.reshape(group_rows, head_count, HD)
    keyset = key_rows.reshape(group_rows, head_count, HD)
    valueset = value_rows.reshape(group_rows, head_count, HD)

    def attend_block(block_index, context):
        first_row = (block_index * QBLK).astype(jnp.int32)
        window_low = jnp.clip(first_row - MAXLEN, 0, group_rows - window)
        query_block = lax.dynamic_slice_in_dim(queries, first_row, QBLK, 0)
        key_block = lax.dynamic_slice_in_dim(keyset, window_low, window, 0)
        value_block = lax.dynamic_slice_in_dim(valueset, window_low, window, 0)
        segment_query = lax.dynamic_slice_in_dim(segment, first_row, QBLK, 0)
        segment_key = lax.dynamic_slice_in_dim(segment, window_low, window, 0)
        allowed = (segment_query[:, None] == segment_key[None, :]) & (segment_key[None, :] >= 0)
        scores = (
            jnp.einsum("qhd,khd->hqk", query_block, key_block, preferred_element_type=jnp.float32)
            * score_scale
        )
        scores = jnp.where(allowed[None], scores, MASKED)
        highest = jnp.max(scores, axis=2, keepdims=True)
        exponentials = jnp.exp(scores - highest)
        denominator = jnp.sum(exponentials, axis=2, keepdims=True)
        weights = (exponentials / denominator).astype(jnp.bfloat16)
        blended = jnp.einsum(
            "hqk,khd->qhd", weights, value_block, preferred_element_type=jnp.float32
        )
        blended = jnp.where((segment_query >= 0)[:, None, None], blended, 0.0).astype(jnp.bfloat16)
        return lax.dynamic_update_slice_in_dim(
            context, blended.reshape(QBLK, width_per_head), first_row, 0
        )

    blocks = (live_count + QBLK - 1) // QBLK
    return lax.fori_loop(
        0, blocks, attend_block, jnp.zeros((group_rows, width_per_head), jnp.bfloat16)
    )


def front(context_rows, carried_rows, out_proj, norm_gain, norm_bias, glu_proj):
    carried = carried_rows.astype(jnp.float32) + jnp.dot(
        context_rows,
        lax.all_gather(out_proj, "mp", axis=1, tiled=True),
        preferred_element_type=jnp.float32,
    )
    average = jnp.mean(carried, axis=1, keepdims=True)
    centred = carried - average
    variance = jnp.mean(centred * centred, axis=1, keepdims=True)
    normed = (centred * lax.rsqrt(variance + EPS) * norm_gain + norm_bias).astype(jnp.bfloat16)
    halves = jnp.dot(
        normed,
        lax.all_gather(glu_proj, "mp", axis=1, tiled=True),
        preferred_element_type=jnp.float32,
    )
    feature_count = halves.shape[1] // 2
    gated_rows = (halves[:, :feature_count] * jax.nn.sigmoid(halves[:, feature_count:])).astype(
        jnp.bfloat16
    )
    return (carried, gated_rows)


def depthwise(gated_rows, segment, conv_taps):
    output_rows = gated_rows.shape[0] - 2 * HALF
    centre = segment[HALF : HALF + output_rows]
    accumulated = jnp.zeros((output_rows, gated_rows.shape[1]), jnp.float32)
    for tap_index in range(KERNEL):
        same_segment = (segment[tap_index : tap_index + output_rows] == centre)[:, None]
        term = jnp.where(
            same_segment, gated_rows[tap_index : tap_index + output_rows].astype(jnp.float32), 0.0
        )
        accumulated = accumulated + term * conv_taps[tap_index]
    return accumulated


def on_device(
    query_rows,
    key_rows,
    value_rows,
    residual,
    lengths,
    assignment,
    out_proj,
    norm_gain,
    norm_bias,
    glu_proj,
    conv_taps,
    batch_scale,
    batch_shift,
    down_proj,
):
    query_flat = unpack_pairs(query_rows)
    key_flat = unpack_pairs(key_rows)
    value_flat = unpack_pairs(value_rows)
    residual_flat = unpack_fours(residual)
    data_group = lax.axis_index("dp")
    slab_index = lax.axis_index("mp")
    groups = lax.axis_size("dp")
    slab_count = lax.axis_size("mp")
    group_rows = query_flat.shape[0]
    slab_rows = group_rows // slab_count
    width_per_head = query_flat.shape[1]
    per_group = lengths.shape[0] // groups
    capacity = PIECES * MAXLEN
    source, before_start, after_start, slot_first = utterance_tables(lengths, assignment, per_group)
    receive_table = source * capacity + slot_first
    segment, occupied_slots, incoming_row = find_frames(
        data_group, assignment, after_start, lengths, group_rows, receive_table
    )
    send_frame, valid_slot = outgoing_rows(
        data_group, groups, per_group, capacity, lengths, assignment, before_start, slot_first
    )
    padded_segment = jnp.pad(segment, (HALF, HALF), constant_values=-2)
    wide_segment = lax.dynamic_slice_in_dim(
        padded_segment, slab_index * slab_rows, slab_rows + 2 * HALF
    )
    centre_segment = wide_segment[HALF : HALF + slab_rows]
    members = [query_flat, key_flat, value_flat, residual_flat]
    stacked = jnp.concatenate(members, axis=1)
    received_rows = lax.all_to_all(
        pack_outgoing(stacked, send_frame, valid_slot),
        "dp",
        split_axis=0,
        concat_axis=0,
        tiled=True,
    )
    balanced_rows = finalize_rows(received_rows, occupied_slots, incoming_row)
    context = attend(
        balanced_rows[:, :width_per_head],
        balanced_rows[:, width_per_head : 2 * width_per_head],
        balanced_rows[:, 2 * width_per_head : 3 * width_per_head],
        segment,
        jnp.sum(occupied_slots.astype(jnp.int32)),
    )
    portion_carried = balanced_rows[:, 3 * width_per_head :]
    context_slab, carried_slab = (
        lax.all_to_all(context, "mp", split_axis=0, concat_axis=1, tiled=True),
        lax.all_to_all(portion_carried, "mp", split_axis=0, concat_axis=1, tiled=True),
    )
    carried, gated_rows = front(
        context_slab, carried_slab, out_proj, norm_gain, norm_bias, glu_proj
    )
    wide_gated = with_halo(gated_rows, (("mp", 0),), HALF)
    convolved = depthwise(wide_gated, wide_segment, conv_taps)
    affine = convolved * batch_scale + batch_shift
    swished = (affine * jax.nn.sigmoid(affine)).astype(jnp.bfloat16)
    lowered = jnp.dot(
        swished,
        lax.all_gather(down_proj, "mp", axis=1, tiled=True),
        preferred_element_type=jnp.float32,
    )
    return jnp.where((centre_segment >= 0)[:, None], carried + lowered, 0.0).astype(jnp.bfloat16)


def solution(mesh):
    in_specs = (
        P("dp", "mp", None),
        P("dp", "mp", None),
        P("dp", "mp", None),
        P("dp", "mp", None),
        P(),
        P(),
        P(None, "mp"),
        P(),
        P(),
        P(None, "mp"),
        P(),
        P(),
        P(),
        P(None, "mp"),
    )
    out_specs = P(("dp", "mp"), None)
    return jax.shard_map(
        on_device, mesh=mesh, in_specs=in_specs, out_specs=out_specs, check_vma=False
    )
```

profile of v0, /device:TPU:4, one launch (start us, length us, event | category | flops | bytes accessed | tf_op | source)
XLA Modules:
  0.0 453.2 jit_solution(10994633186165721107)
XLA Ops:
  6.5 0.7 all-gather.4.cloned.1.call-update
  7.3 0.7 all-gather.6.cloned.1.call-update
  8.0 2.4 copy.61
  10.5 1.5 copy.62
  12.0 1.0 reshape.217
  13.0 3.7 copy.63
  16.7 4.5 %copy.64 = bf16[2048,2,2,64]{3,2,1,0:T(2,128)(2,1)S(1)} copy(bf16[2048,2,2,64]{0,3,1,2:T(8,128)(2,1)} %bitcast.38) | data formatting | bytes 2097152 | tf_op jit(solution)/shard_map/transpose | solution.py:38
  21.2 1.8 reshape.219
  23.0 3.7 copy.65
  26.7 4.5 copy.66
  31.2 1.8 reshape.221
  33.0 3.6 reshape_transpose_reshape.3
  37.2 4.5 pad_maximum_fusion
  41.7 21.2 %gather_fusion = bf16[4096,576]{1,0:T(8,128)(2,1)} fusion(bf16[4096,576]{1,0:T(8,128)(2,1)} %pad_maximum_fusion, s32[4096]{0:T(1024)S(1)} %fusion.80), kind=kCustom, calls=%fused_computation.clone | custom fusion | bytes 9453568 | tf_op jit(solution)/shard_map/jit(_take)/gather | solution.py:109
  63.0 5.8 %select_select_fusion.1 = bf16[4096,576]{1,0:T(8,128)(2,1)} fusion(bf16[4096,576]{1,0:T(8,128)(2,1)} %gather_fusion, pred[4096]{0:T(1024)(128)(4,1)S(1)} %compare_and_fusion.5, pred[4096]{0:T(1024)(128)(4,1)S(1)} %fusion.85), kind=kLoop, calls=%fused_computation.59 | loop fusion | flops 4718592 | bytes 9445376 | tf_op jit(solution)/shard_map/jit(_where)/select_n | solution.py:110
  68.9 7.7 %copy.67 = bf16[4,1024,576]{1,2,0:T(8,128)(2,1)} copy(bf16[4,1024,576]{2,1,0:T(8,128)(2,1)} %bitcast.35) | data formatting | bytes 9437184 | tf_op jit(solution)/shard_map/all_to_all | solution.py:238
  76.5 5.1 %all-to-all-start = ((bf16[4,1024,576]{1,2,0:T(8,128)(2,1)}), bf16[4,1024,576]{1,2,0:T(8,128)(2,1)}, u32[]{:S(2)}, u32[]{:S(2)}) async-start(bf16[4,1024,576]{1,2,0:T(8,128)(2,1)} %copy.67), calls=%async_computation | async-start | bytes 9437184 | tf_op jit(solution)/shard_map/all_to_all | solution.py:238
  84.0 48.8 %all-to-all-done = bf16[4,1024,576]{1,2,0:T(8,128)(2,1)} async-done(((bf16[4,1024,576]{1,2,0:T(8,128)(2,1)}), bf16[4,1024,576]{1,2,0:T(8,128)(2,1)}, u32[]{:S(2)}, u32[]{:S(2)}) %all-to-all-start) | async-done | bytes 4718624 | tf_op jit(solution)/shard_map/all_to_all | solution.py:238
  132.8 7.7 %copy.68 = bf16[4,1024,576]{2,1,0:T(8,128)(2,1)} copy(bf16[4,1024,576]{1,2,0:T(8,128)(2,1)} %all-to-all-done) | data formatting | bytes 9437184 | tf_op jit(solution)/shard_map/all_to_all | solution.py:238
  140.5 21.2 %gather_fusion.1 = bf16[4096,576]{1,0:T(8,128)(2,1)} fusion(bf16[4096,576]{1,0:T(8,128)(2,1)} %bitcast.33, s32[4096]{0:T(1024)S(1)} %get-tuple-element.200), kind=kCustom, calls=%fused_computation.1.clone | custom fusion | bytes 9453568 | tf_op jit(solution)/shard_map/jit(_take)/gather | solution.py:114
  161.7 5.6 %select_select_fusion = bf16[4096,576]{1,0:T(8,128)(2,1)S(1)} fusion(bf16[4096,576]{1,0:T(8,128)(2,1)} %gather_fusion.1, pred[4096]{0:T(1024)(128)(4,1)S(1)} %compare_and_fusion.4, pred[4096]{0:T(1024)(128)(4,1)S(1)} %fusion.71), kind=kLoop, calls=%fused_computation.58 | loop fusion | flops 4718592 | bytes 9445376 | tf_op jit(solution)/shard_map/jit(_where)/select_n | solution.py:115
  167.8 1.8 copy-done
  169.7 1.3 copy.70
  171.0 1.3 copy.71
  173.0 67.8 %while.12 = (s32[]{:T(128)}, bf16[4096,128]{1,0:T(8,128)(2,1)S(1)}, s32[]{:T(128)}, s32[4096]{0:T(1024)S(1)}, bf16[4096,2,64]{0,2,1:T(8,128)(2,1)}, /*index=5*/b...) while((s32[]{:T(128)}, bf16[4096,128]{1,0:T(8,128)(2,1)S(1)}, ...), condition=%wide.region_12.14_spmd, body=%wide.region_9.13_spmd.sunk | while | flops 275909120 | bytes 10777831 | solution.py:154
  173.7 4.6 %fusion.112 = (f32[2,512]{1,0:T(2,128)S(1)}, f32[2,512,1024]{2,1,0:T(8,128)}) fusion(pred[512,1024]{1,0:T(8,128)(4,1)S(1)} %compare_and_fusion.7, bf16[4096,2,64]{0,2,1:T(8,128)(2,1)S(1)} %get-tuple-element.298, s32[]{:T(128)S(6)} %min.8, bf16[4096,2,64]{0,2,1:T(8,128)(2,1)} %get-tuple-element.297, s32[]{:T(128)S(6)} %select_n.445), kind=kOutput, calls=%fused_computation.236.clone.1 | convolution fusion | flops 138413056 | bytes 5115912 | tf_op jit(solution)/shard_map/while/body/sub | solution.py:142
  178.3 3.1 fusion.113
  182.2 4.6 %fusion.112 = (f32[2,512]{1,0:T(2,128)S(1)}, f32[2,512,1024]{2,1,0:T(8,128)}) fusion(pred[512,1024]{1,0:T(8,128)(4,1)S(1)} %compare_and_fusion.7, bf16[4096,2,64]{0,2,1:T(8,128)(2,1)S(1)} %get-tuple-element.298, s32[]{:T(128)S(6)} %min.8, bf16[4096,2,64]{0,2,1:T(8,128)(2,1)} %get-tuple-element.297, s32[]{:T(128)S(6)} %select_n.445), kind=kOutput, calls=%fused_computation.236.clone.1 | convolution fusion | flops 138413056 | bytes 5115912 | tf_op jit(solution)/shard_map/while/body/sub | solution.py:142
  186.7 3.2 fusion.113
  190.7 4.6 %fusion.112 = (f32[2,512]{1,0:T(2,128)S(1)}, f32[2,512,1024]{2,1,0:T(8,128)}) fusion(pred[512,1024]{1,0:T(8,128)(4,1)S(1)} %compare_and_fusion.7, bf16[4096,2,64]{0,2,1:T(8,128)(2,1)S(1)} %get-tuple-element.298, s32[]{:T(128)S(6)} %min.8, bf16[4096,2,64]{0,2,1:T(8,128)(2,1)} %get-tuple-element.297, s32[]{:T(128)S(6)} %select_n.445), kind=kOutput, calls=%fused_computation.236.clone.1 | convolution fusion | flops 138413056 | bytes 5115912 | tf_op jit(solution)/shard_map/while/body/sub | solution.py:142
  195.2 3.1 fusion.113
  199.1 4.6 %fusion.112 = (f32[2,512]{1,0:T(2,128)S(1)}, f32[2,512,1024]{2,1,0:T(8,128)}) fusion(pred[512,1024]{1,0:T(8,128)(4,1)S(1)} %compare_and_fusion.7, bf16[4096,2,64]{0,2,1:T(8,128)(2,1)S(1)} %get-tuple-element.298, s32[]{:T(128)S(6)} %min.8, bf16[4096,2,64]{0,2,1:T(8,128)(2,1)} %get-tuple-element.297, s32[]{:T(128)S(6)} %select_n.445), kind=kOutput, calls=%fused_computation.236.clone.1 | convolution fusion | flops 138413056 | bytes 5115912 | tf_op jit(solution)/shard_map/while/body/sub | solution.py:142
  203.7 3.1 fusion.113
  207.6 4.6 %fusion.112 = (f32[2,512]{1,0:T(2,128)S(1)}, f32[2,512,1024]{2,1,0:T(8,128)}) fusion(pred[512,1024]{1,0:T(8,128)(4,1)S(1)} %compare_and_fusion.7, bf16[4096,2,64]{0,2,1:T(8,128)(2,1)S(1)} %get-tuple-element.298, s32[]{:T(128)S(6)} %min.8, bf16[4096,2,64]{0,2,1:T(8,128)(2,1)} %get-tuple-element.297, s32[]{:T(128)S(6)} %select_n.445), kind=kOutput, calls=%fused_computation.236.clone.1 | convolution fusion | flops 138413056 | bytes 5115912 | tf_op jit(solution)/shard_map/while/body/sub | solution.py:142
  212.1 3.1 fusion.113
  216.0 4.6 %fusion.112 = (f32[2,512]{1,0:T(2,128)S(1)}, f32[2,512,1024]{2,1,0:T(8,128)}) fusion(pred[512,1024]{1,0:T(8,128)(4,1)S(1)} %compare_and_fusion.7, bf16[4096,2,64]{0,2,1:T(8,128)(2,1)S(1)} %get-tuple-element.298, s32[]{:T(128)S(6)} %min.8, bf16[4096,2,64]{0,2,1:T(8,128)(2,1)} %get-tuple-element.297, s32[]{:T(128)S(6)} %select_n.445), kind=kOutput, calls=%fused_computation.236.clone.1 | convolution fusion | flops 138413056 | bytes 5115912 | tf_op jit(solution)/shard_map/while/body/sub | solution.py:142
  220.6 3.1 fusion.113
  224.5 4.6 %fusion.112 = (f32[2,512]{1,0:T(2,128)S(1)}, f32[2,512,1024]{2,1,0:T(8,128)}) fusion(pred[512,1024]{1,0:T(8,128)(4,1)S(1)} %compare_and_fusion.7, bf16[4096,2,64]{0,2,1:T(8,128)(2,1)S(1)} %get-tuple-element.298, s32[]{:T(128)S(6)} %min.8, bf16[4096,2,64]{0,2,1:T(8,128)(2,1)} %get-tuple-element.297, s32[]{:T(128)S(6)} %select_n.445), kind=kOutput, calls=%fused_computation.236.clone.1 | convolution fusion | flops 138413056 | bytes 5115912 | tf_op jit(solution)/shard_map/while/body/sub | solution.py:142
  229.0 3.1 fusion.113
  232.9 4.6 %fusion.112 = (f32[2,512]{1,0:T(2,128)S(1)}, f32[2,512,1024]{2,1,0:T(8,128)}) fusion(pred[512,1024]{1,0:T(8,128)(4,1)S(1)} %compare_and_fusion.7, bf16[4096,2,64]{0,2,1:T(8,128)(2,1)S(1)} %get-tuple-element.298, s32[]{:T(128)S(6)} %min.8, bf16[4096,2,64]{0,2,1:T(8,128)(2,1)} %get-tuple-element.297, s32[]{:T(128)S(6)} %select_n.445), kind=kOutput, calls=%fused_computation.236.clone.1 | convolution fusion | flops 138413056 | bytes 5115912 | tf_op jit(solution)/shard_map/while/body/sub | solution.py:142
  237.5 3.1 fusion.113
  240.8 1.0 copy-done.1
  241.8 7.5 %all-to-all-start.2 = ((bf16[8,512,128]{2,1,0:T(8,128)(2,1)}), bf16[8,512,128]{2,1,0:T(8,128)(2,1)S(1)}, u32[]{:S(2)}, u32[]{:S(2)}) async-start(bf16[8,512,128]{2,1,0:T(8,128)(2,1)} %bitcast.41), calls=%async_computation.2 | async-start | bytes 2097152 | tf_op jit(solution)/shard_map/all_to_all | solution.py:255
  249.3 0.7 all-gather.8.cloned.1.call-update
  250.0 2.3 copy.69
  252.3 37.5 %all-to-all-done.2 = bf16[8,512,128]{2,1,0:T(8,128)(2,1)S(1)} async-done(((bf16[8,512,128]{2,1,0:T(8,128)(2,1)}), bf16[8,512,128]{2,1,0:T(8,128)(2,1)S(1)}, u32[]{:S(2)}, u32[]{:S(2)}) %all-to-all-start.2) | async-done | bytes 1048608 | tf_op jit(solution)/shard_map/all_to_all | solution.py:255
  289.8 4.3 all-to-all-start.1
  294.2 0.9 slice_reduce_fusion.30
  295.7 0.7 slice_compare_fusion.28
  296.4 0.7 slice_compare_fusion.27
  297.1 0.7 slice_compare_fusion.29
  297.8 1.4 copy.74
  299.1 62.0 %all-to-all-done.1 = bf16[8,512,192]{1,2,0:T(8,128)(2,1)} async-done(((bf16[8,512,192]{1,2,0:T(8,128)(2,1)}), bf16[8,512,192]{1,2,0:T(8,128)(2,1)}, u32[]{:S(2)}, u32[]{:S(2)}) %all-to-all-start.1) | async-done | bytes 1572896 | tf_op jit(solution)/shard_map/all_to_all | solution.py:256
  361.2 1.8 convert_element_type.172
  363.0 2.3 copy.75
  365.3 5.1 %fusion.98 = (f32[512]{0:T(512)S(1)}, f32[512,1536]{1,0:T(8,128)S(1)}) fusion(f32[512,1536]{1,0:T(8,128)} %copy.75, bf16[512,1024]{0,1:T(8,128)(2,1)} %bitcast.46, bf16[1024,1536]{0,1:T(8,128)(2,1)} %all-gather.4.cloned.1.call-done), kind=kOutput, calls=%fused_computation.240 | convolution fusion | flops 1612185088 | bytes 10487808 | tf_op jit(solution)/shard_map/dot_general | solution.py:160
  371.1 7.7 %fusion.36 = f32[512,3072]{1,0:T(8,128)S(1)} fusion(bf16[1536,3072]{1,0:T(8,128)(2,1)} %all-gather.6.cloned.1.call-done, f32[512,1536]{1,0:T(8,128)S(1)} %get-tuple-element.207, f32[1536]{0:T(1024)S(1)} %copy-done.7, f32[1536]{0:T(1024)S(1)} %copy-done.8, f32[512]{0:T(512)S(1)} %add_rsqrt_fusion, f32[512]{0:T(512)S(1)} %broadcast_multiply_fusion), kind=kOutput, calls=%fused_computation.73 | convolution fusion | flops 4835770368 | bytes 18890752 | tf_op jit(solution)/shard_map/dot_general | solution.py:169
  378.8 0.8 fusion.34
  379.7 1.1 copy-done.2
  380.9 4.3 collective-permute-start
  385.2 1.5 collective-permute-start.1
  386.7 0.8 slice_reduce_fusion.29
  387.5 3.8 collective-permute-done.1
  391.2 55.4 %fusion.35 = bf16[512,1536]{1,0:T(8,128)(2,1)} fusion(f32[512,1536]{1,0:T(8,128)S(1)} %get-tuple-element.207, bf16[1536,1536]{0,1:T(8,128)(2,1)} %all-gather.8.cloned.1.call-done, pred[512]{0:T(512)(128)(4,1)} %get-tuple-element.176, bf16[512,1536]{1,0:T(8,128)(2,1)} %copy-done.2, bf16[15,1536]{1,0:T(8,128)(2,1)} %collective-permute-done.1, ...), kind=kOutput, calls=%fused_computation.72 | convolution fusion | flops 2590507008 | bytes 11320832 | tf_op jit(solution)/shard_map/dot_general | solution.py:265
  (88 shorter events, 10.8 us)
Async XLA Ops:
  6.5 358.8 %all-gather.4.cloned.1.call-start = ((), (), s32[]{:S(2)}) async-start(), calls=%async_computation.3 | async-start | bytes 3538944 | tf_op jit(solution)/shard_map/all_gather | solution.py:162
  7.3 363.7 %all-gather.6.cloned.1.call-start = ((), (), s32[]{:S(2)}) async-start(), calls=%async_computation.4 | async-start | bytes 10616832 | tf_op jit(solution)/shard_map/all_gather | solution.py:171
  31.2 5.4 %copy-start.6 = (s32[64]{0:T(128)S(1)}, s32[64]{0:T(128)}, u32[]{:S(2)}) copy-start(s32[64]{0:T(128)} %param.23) | copy-start | bytes 772
  31.2 5.5 %copy-start.5 = (s32[64]{0:T(128)S(1)}, s32[64]{0:T(128)}, u32[]{:S(2)}) copy-start(s32[64]{0:T(128)} %param.22) | copy-start | bytes 772
  76.5 56.2 %all-to-all-start = ((bf16[4,1024,576]{1,2,0:T(8,128)(2,1)}), bf16[4,1024,576]{1,2,0:T(8,128)(2,1)}, u32[]{:S(2)}, u32[]{:S(2)}) async-start(bf16[4,1024,576]{1,2,0:T(8,128)(2,1)} %copy.67), calls=%async_computation | async-start | bytes 9437184 | tf_op jit(solution)/shard_map/all_to_all | solution.py:238
  167.3 2.4 copy-start
  240.8 1.0 copy-start.1
  241.8 8.3 %slice-start = ((bf16[4096,576]{1,0:T(8,128)(2,1)}), bf16[4096,192]{1,0:T(8,128)(2,1)S(1)}, s32[]{:S(2)}) async-start(bf16[4096,576]{1,0:T(8,128)(2,1)} %copy-done), calls=%async_computation.6 | async-start | bytes 4194304 | tf_op jit(solution)/shard_map/slice | solution.py:253
  241.8 48.1 %all-to-all-start.2 = ((bf16[8,512,128]{2,1,0:T(8,128)(2,1)}), bf16[8,512,128]{2,1,0:T(8,128)(2,1)S(1)}, u32[]{:S(2)}, u32[]{:S(2)}) async-start(bf16[8,512,128]{2,1,0:T(8,128)(2,1)} %bitcast.41), calls=%async_computation.2 | async-start | bytes 2097152 | tf_op jit(solution)/shard_map/all_to_all | solution.py:255
  249.3 138.2 %all-gather.8.cloned.1.call-start = ((), (), s32[]{:S(2)}) async-start(), calls=%async_computation.5 | async-start | bytes 5308416 | tf_op jit(solution)/shard_map/all_gather | solution.py:267
  250.0 44.2 %copy-start.3 = (f32[31,1536]{1,0:T(8,128)S(1)}, f32[31,1536]{1,0:T(8,128)}, u32[]{:S(2)}) copy-start(f32[31,1536]{1,0:T(8,128)} %param.28) | copy-start | bytes 571396
  289.8 71.3 %all-to-all-start.1 = ((bf16[8,512,192]{1,2,0:T(8,128)(2,1)}), bf16[8,512,192]{1,2,0:T(8,128)(2,1)}, u32[]{:S(2)}, u32[]{:S(2)}) async-start(bf16[8,512,192]{1,2,0:T(8,128)(2,1)} %copy.69), calls=%async_computation.1 | async-start | bytes 3145728 | tf_op jit(solution)/shard_map/all_to_all | solution.py:256
  370.4 0.7 copy-start.7
  370.4 0.7 copy-start.8
  378.8 12.4 %copy-start.4 = (f32[1536]{0:T(1024)S(1)}, f32[1536]{0:T(1024)}, u32[]{:S(2)}) copy-start(f32[1536]{0:T(1024)} %get-tuple-element.119) | copy-start | bytes 18436
  379.7 1.2 copy-start.2
  380.9 6.6 %collective-permute-start = (bf16[15,1536]{1,0:T(8,128)(2,1)S(1)}, bf16[15,1536]{1,0:T(8,128)(2,1)}, u32[]{:S(2)}, u32[]{:S(2)}) collective-permute-start(bf16[15,1536]{1,0:T(8,128)(2,1)S(1)} %get-tuple-element.165), channel_id=1, source_target_pairs={{0,1},{1,2},{2,3},{3,4},{4,5},{5,6},{6,7},{8,9},{9,10},{10,11},{11... | collective-permute-start | bytes 138248 | tf_op jit(solution)/shard_map/ppermute | solution.py:24
  385.2 6.1 %collective-permute-start.1 = (bf16[15,1536]{1,0:T(8,128)(2,1)S(1)}, bf16[15,1536]{1,0:T(8,128)(2,1)}, u32[]{:S(2)}, u32[]{:S(2)}) collective-permute-start(bf16[15,1536]{1,0:T(8,128)(2,1)S(1)} %get-tuple-element.166), channel_id=1, source_target_pairs={{1,0},{2,1},{3,2},{4,3},{5,4},{6,5},{7,6},{9,8},{10,9},{11,10},{12... | collective-permute-start | bytes 138248 | tf_op jit(solution)/shard_map/ppermute | solution.py:26
Sparse Core Ops, SparseCore 0:
  9.5 61.2 all-gather.3
  72.8 136.4 all-gather.5
  252.3 116.2 all-gather.7
where the time goes:
time: 455 us; the launch traced here: 453 us
  waiting for transfers between devices  154 us (34%)
  matrix products  130 us (29%)
  local copies, waits for them, and re-layouts  103 us (23%)
  other arithmetic  28.5 us (6%)
  starting transfers between devices  22.8 us (5%)
  between operations  14.1 us (3%)
    all_to_all x1, waiting for transfers between devices, on_device(): lax.all_to_all(portion_carried, 'mp', split_axis=0, concat_axis=1, tiled=...  62 us
    dot_general x1, matrix products, on_device(): jnp.dot(swished, lax.all_gather(down_proj, 'mp', axis=1, tiled=True), pre...  55.4 us
    all_to_all x1, waiting for transfers between devices, on_device(): lax.all_to_all(pack_outgoing(stacked, send_frame, valid_slot), 'dp', spli...  48.8 us
    all_to_all x1, waiting for transfers between devices, on_device(): lax.all_to_all(context, 'mp', split_axis=0, concat_axis=1, tiled=True)  37.5 us
    sub x8, matrix products, attend_block(): exponentials = jnp.exp(scores - highest)  36.5 us
    dot_general x8, matrix products, attend_block(): jnp.einsum('hqk,khd->qhd', weights, value_block, preferred_element_type=j...  25.1 us
    gather x1, local copies, waits for them, and re-layouts, finalize_rows(): picked = jnp.take(received_rows, incoming_row, axis=0)  21.2 us
    gather x1, local copies, waits for them, and re-layouts, pack_outgoing(): picked = jnp.take(stacked, send_frame, axis=0)  21.2 us
  transfers between devices with their start and end apart: 8, of which 4 were waited for; matrix products, arithmetic and copies ran while one was open for 45% of the time, Pallas kernels for 0%

commit v1 on v0

--- a/solution.py
+++ b/solution.py
@@ -2,6 +2,7 @@
 import jax.numpy as jnp
 from jax import lax
 from jax.sharding import PartitionSpec as P
+from jax.lax import all_to_all, axis_size
 
 HD = 64
 KERNEL = 31
@@ -253,7 +254,10 @@
     portion_carried = balanced_rows[:, 3 * width_per_head :]
     context_slab, carried_slab = (
         lax.all_to_all(context, "mp", split_axis=0, concat_axis=1, tiled=True),
-        lax.all_to_all(portion_carried, "mp", split_axis=0, concat_axis=1, tiled=True),
+        jnp.concatenate(
+            all_to_all(jnp.stack(jnp.split(portion_carried, axis_size("mp"), axis=0)), "mp", 0, 0),
+            axis=1,
+        ),
     )
     carried, gated_rows = front(
         context_slab, carried_slab, out_proj, norm_gain, norm_bias, glu_proj

time: 455 us -> 437 us (0.960)
  waiting for transfers between devices: 154 us -> 132 us
  local copies, waits for them, and re-layouts: 103 us -> 115 us
  matrix products: 130 us -> 123 us
    all_to_all x1, waiting for transfers between devices: 62 us -> 45.2 us  [on_device(): all_to_all(jnp.stack(jnp.split(portion_carried, axis_size('mp'), axis=0))...]
    sub x8, matrix products: 36.5 us -> 29.2 us  [attend_block(): exponentials = jnp.exp(scores - highest)]
    unnamed x21 -> x26, local copies, waits for them, and re-layouts: 14 us -> 19.8 us
    dynamic_update_slice x16, local copies, waits for them, and re-layouts: 1.16 us -> 6.27 us  [attend_block(): lax.dynamic_update_slice_in_dim(context, blended.reshape(QBLK, width_per_...]
  transfers between devices with their start and end apart: 8 -> 8, of which waited for: 4 -> 4; matrix products, arithmetic and copies ran while one was open for 45% -> 48% of each run, Pallas kernels for 0% -> 0%
where the time goes in v1:
time: 437 us; the launch traced here: 435 us
  waiting for transfers between devices  132 us (30%)
  matrix products  123 us (28%)
  local copies, waits for them, and re-layouts  115 us (26%)
  other arithmetic  28.5 us (7%)
  starting transfers between devices  21.9 us (5%)
  between operations  14.1 us (3%)
    dot_general x1, matrix products, on_device(): jnp.dot(swished, lax.all_gather(down_proj, 'mp', axis=1, tiled=True), pre...  55.4 us
    all_to_all x1, waiting for transfers between devices, on_device(): lax.all_to_all(pack_outgoing(stacked, send_frame, valid_slot), 'dp', spli...  48.1 us
    all_to_all x1, waiting for transfers between devices, on_device(): all_to_all(jnp.stack(jnp.split(portion_carried, axis_size('mp'), axis=0))...  45.2 us
    all_to_all x1, waiting for transfers between devices, on_device(): lax.all_to_all(context, 'mp', split_axis=0, concat_axis=1, tiled=True)  33.1 us
    sub x8, matrix products, attend_block(): exponentials = jnp.exp(scores - highest)  29.2 us
    dot_general x8, matrix products, attend_block(): jnp.einsum('hqk,khd->qhd', weights, value_block, preferred_element_type=j...  25.3 us
    gather x1, local copies, waits for them, and re-layouts, finalize_rows(): picked = jnp.take(received_rows, incoming_row, axis=0)  21.2 us
    gather x1, local copies, waits for them, and re-layouts, pack_outgoing(): picked = jnp.take(stacked, send_frame, axis=0)  21.2 us
  transfers between devices with their start and end apart: 8, of which 4 were waited for; matrix products, arithmetic and copies ran while one was open for 48% of the time, Pallas kernels for 0%

profile of v1, /device:TPU:4, one launch (start us, length us, event | category | flops | bytes accessed | tf_op | source)
XLA Modules:
  0.0 435.0 jit_solution(17416700312984460316)
XLA Ops:
  8.0 2.4 copy.61
  10.5 1.5 copy.62
  12.0 1.0 reshape.216
  13.0 3.7 copy.63
  16.7 4.5 %copy.64 = bf16[2048,2,2,64]{3,2,1,0:T(2,128)(2,1)S(1)} copy(bf16[2048,2,2,64]{0,3,1,2:T(8,128)(2,1)} %bitcast.68) | data formatting | bytes 2097152 | tf_op jit(solution)/shard_map/transpose | solution.py:39
  21.2 1.8 reshape.218
  23.0 3.7 copy.65
  26.7 4.5 %copy.66 = bf16[2048,2,2,64]{3,2,1,0:T(2,128)(2,1)S(1)} copy(bf16[2048,2,2,64]{0,3,1,2:T(8,128)(2,1)} %bitcast.69) | data formatting | bytes 2097152 | tf_op jit(solution)/shard_map/transpose | solution.py:39
  31.2 1.8 reshape.220
  33.0 3.6 reshape_transpose_reshape.3
  37.2 4.5 %pad_maximum_fusion = bf16[4096,576]{1,0:T(8,128)(2,1)} fusion(bf16[4096,192]{1,0:T(8,128)(2,1)S(1)} %reshape_transpose_reshape.3, bf16[4096,128]{1,0:T(8,128)(2,1)} %reshape.220, bf16[4096,128]{1,0:T(8,128)(2,1)} %reshape.218, bf16[4096,128]{1,0:T(8,128)(2,1)S(1)} %reshape.216), kind=kLoop, calls=%fused_computation.57 | loop fusion | flops 18874368 | bytes 9437184 | tf_op jit(solution)/shard_map/concatenate | solution.py:238
  41.7 21.2 %gather_fusion = bf16[4096,576]{1,0:T(8,128)(2,1)} fusion(bf16[4096,576]{1,0:T(8,128)(2,1)} %pad_maximum_fusion, s32[4096]{0:T(1024)S(1)} %fusion.88), kind=kCustom, calls=%fused_computation.clone | custom fusion | bytes 9453568 | tf_op jit(solution)/shard_map/jit(_take)/gather | solution.py:110
  63.0 5.8 %select_select_fusion.1 = bf16[4096,576]{1,0:T(8,128)(2,1)} fusion(bf16[4096,576]{1,0:T(8,128)(2,1)} %gather_fusion, pred[4096]{0:T(1024)(128)(4,1)S(1)} %compare_and_fusion.5, pred[4096]{0:T(1024)(128)(4,1)S(1)} %fusion.93), kind=kLoop, calls=%fused_computation.59 | loop fusion | flops 4718592 | bytes 9445376 | tf_op jit(solution)/shard_map/jit(_where)/select_n | solution.py:111
  68.9 7.7 %copy.67 = bf16[4,1024,576]{1,2,0:T(8,128)(2,1)} copy(bf16[4,1024,576]{2,1,0:T(8,128)(2,1)} %bitcast.65) | data formatting | bytes 9437184 | tf_op jit(solution)/shard_map/all_to_all | solution.py:239
  76.5 5.1 %all-to-all-start = ((bf16[4,1024,576]{1,2,0:T(8,128)(2,1)}), bf16[4,1024,576]{1,2,0:T(8,128)(2,1)}, u32[]{:S(2)}, u32[]{:S(2)}) async-start(bf16[4,1024,576]{1,2,0:T(8,128)(2,1)} %copy.67), calls=%async_computation | async-start | bytes 9437184 | tf_op jit(solution)/shard_map/all_to_all | solution.py:239
  84.7 48.1 %all-to-all-done = bf16[4,1024,576]{1,2,0:T(8,128)(2,1)} async-done(((bf16[4,1024,576]{1,2,0:T(8,128)(2,1)}), bf16[4,1024,576]{1,2,0:T(8,128)(2,1)}, u32[]{:S(2)}, u32[]{:S(2)}) %all-to-all-start) | async-done | bytes 4718624 | tf_op jit(solution)/shard_map/all_to_all | solution.py:239
  132.8 7.7 %copy.68 = bf16[4,1024,576]{2,1,0:T(8,128)(2,1)} copy(bf16[4,1024,576]{1,2,0:T(8,128)(2,1)} %all-to-all-done) | data formatting | bytes 9437184 | tf_op jit(solution)/shard_map/all_to_all | solution.py:239
  140.5 21.2 %gather_fusion.1 = bf16[4096,576]{1,0:T(8,128)(2,1)} fusion(bf16[4096,576]{1,0:T(8,128)(2,1)} %bitcast.64, s32[4096]{0:T(1024)S(1)} %get-tuple-element.200), kind=kCustom, calls=%fused_computation.1.clone | custom fusion | bytes 9453568 | tf_op jit(solution)/shard_map/jit(_take)/gather | solution.py:115
  161.7 5.6 %select_select_fusion = bf16[4096,576]{1,0:T(8,128)(2,1)S(1)} fusion(bf16[4096,576]{1,0:T(8,128)(2,1)} %gather_fusion.1, pred[4096]{0:T(1024)(128)(4,1)S(1)} %compare_and_fusion.4, pred[4096]{0:T(1024)(128)(4,1)S(1)} %fusion.79), kind=kLoop, calls=%fused_computation.58 | loop fusion | flops 4718592 | bytes 9445376 | tf_op jit(solution)/shard_map/jit(_where)/select_n | solution.py:116
  167.8 1.8 copy-done
  169.7 1.3 copy.70
  172.0 1.1 broadcast_in_dim.379.clone
  173.2 65.5 %while.12 = (s32[]{:T(128)}, bf16[4096,128]{1,0:T(8,128)(2,1)}, s32[]{:T(128)}, s32[4096]{0:T(1024)S(1)}, bf16[4096,2,64]{0,2,1:T(8,128)(2,1)}, /*index=5*/bf16[...) while((s32[]{:T(128)}, bf16[4096,128]{1,0:T(8,128)(2,1)}, ...), condition=%wide.region_12.14_spmd, body=%wide.region_9.13_spmd.sunk | while | flops 275909120 | bytes 10777831 | solution.py:155
  173.7 3.7 fusion.120
  177.4 3.1 fusion.121
  181.9 3.7 fusion.120
  185.5 3.2 fusion.121
  190.1 3.7 fusion.120
  193.8 3.1 fusion.121
  198.2 3.7 fusion.120
  201.9 3.1 fusion.121
  206.4 3.7 fusion.120
  210.0 3.1 fusion.121
  214.5 3.7 fusion.120
  218.2 3.3 fusion.121
  222.9 3.7 fusion.120
  226.5 3.2 fusion.121
  231.0 3.7 fusion.120
  234.7 3.1 fusion.121
  238.6 7.1 %all-to-all-start.2 = ((bf16[8,512,128]{2,1,0:T(8,128)(2,1)}), bf16[8,512,128]{2,1,0:T(8,128)(2,1)S(1)}, u32[]{:S(2)}, u32[]{:S(2)}) async-start(bf16[8,512,128]{2,1,0:T(8,128)(2,1)} %bitcast.23), calls=%async_computation.2 | async-start | bytes 2097152 | tf_op jit(solution)/shard_map/all_to_all | solution.py:256
  245.7 1.0 fusion.78
  246.7 1.0 fusion.77
  247.7 1.0 fusion.76
  248.6 1.0 fusion.75
  249.6 1.0 fusion.74
  250.6 1.0 fusion.73
  251.6 1.0 fusion.72
  252.5 1.0 fusion.71
  253.5 2.3 copy.69
  255.8 33.1 %all-to-all-done.2 = bf16[8,512,128]{2,1,0:T(8,128)(2,1)S(1)} async-done(((bf16[8,512,128]{2,1,0:T(8,128)(2,1)}), bf16[8,512,128]{2,1,0:T(8,128)(2,1)S(1)}, u32[]{:S(2)}, u32[]{:S(2)}) %all-to-all-start.2) | async-done | bytes 1048608 | tf_op jit(solution)/shard_map/all_to_all | solution.py:256
  288.9 4.3 all-to-all-start.1
  293.3 0.9 slice_reduce_fusion.30
  296.9 1.4 copy.74
  298.3 45.2 %all-to-all-done.1 = bf16[8,512,192]{1,2,0:T(8,128)(2,1)} async-done(((bf16[8,512,192]{1,2,0:T(8,128)(2,1)}), bf16[8,512,192]{1,2,0:T(8,128)(2,1)}, u32[]{:S(2)}, u32[]{:S(2)}) %all-to-all-start.1) | async-done | bytes 1572896 | tf_op jit(solution)/shard_map/all_to_all | solution.py:258
  343.5 1.8 convert_element_type.172
  345.3 2.3 copy.75
  347.6 5.1 %fusion.106 = (f32[512]{0:T(512)S(1)}, f32[512,1536]{1,0:T(8,128)S(1)}) fusion(f32[512,1536]{1,0:T(8,128)} %copy.75, bf16[512,1024]{0,1:T(8,128)(2,1)} %bitcast.75, bf16[1024,1536]{0,1:T(8,128)(2,1)} %all-gather.4.cloned.1.call-done), kind=kOutput, calls=%fused_computation.256 | convolution fusion | flops 1612185088 | bytes 10487808 | tf_op jit(solution)/shard_map/dot_general | solution.py:161
  353.4 7.7 %fusion.36 = f32[512,3072]{1,0:T(8,128)S(1)} fusion(bf16[1536,3072]{1,0:T(8,128)(2,1)} %all-gather.6.cloned.1.call-done, f32[512,1536]{1,0:T(8,128)S(1)} %get-tuple-element.207, f32[1536]{0:T(1024)S(1)} %copy-done.6, f32[1536]{0:T(1024)S(1)} %copy-done.7, f32[512]{0:T(512)S(1)} %add_rsqrt_fusion, f32[512]{0:T(512)S(1)} %broadcast_multiply_fusion), kind=kOutput, calls=%fused_computation.73 | convolution fusion | flops 4835770368 | bytes 18890752 | tf_op jit(solution)/shard_map/dot_general | solution.py:170
  361.1 0.8 fusion.34
  362.0 1.1 copy-done.1
  363.2 3.8 collective-permute-start
  367.0 1.5 collective-permute-start.1
  369.3 3.8 collective-permute-done.1
  373.1 55.4 %fusion.35 = bf16[512,1536]{1,0:T(8,128)(2,1)} fusion(f32[512,1536]{1,0:T(8,128)S(1)} %get-tuple-element.207, bf16[1536,1536]{0,1:T(8,128)(2,1)} %all-gather.8.cloned.1.call-done, pred[512]{0:T(512)(128)(4,1)} %get-tuple-element.176, bf16[512,1536]{1,0:T(8,128)(2,1)} %copy-done.1, bf16[15,1536]{1,0:T(8,128)(2,1)} %collective-permute-done.1, ...), kind=kOutput, calls=%fused_computation.72 | convolution fusion | flops 2590507008 | bytes 11320832 | tf_op jit(solution)/shard_map/dot_general | solution.py:269
  (92 shorter events, 21.2 us)
Async XLA Ops:
  6.5 341.1 %all-gather.4.cloned.1.call-start = ((), (), s32[]{:S(2)}) async-start(), calls=%async_computation.3 | async-start | bytes 3538944 | tf_op jit(solution)/shard_map/all_gather | solution.py:163
  7.3 346.0 %all-gather.6.cloned.1.call-start = ((), (), s32[]{:S(2)}) async-start(), calls=%async_computation.4 | async-start | bytes 10616832 | tf_op jit(solution)/shard_map/all_gather | solution.py:172
  31.2 5.4 %copy-start.5 = (s32[64]{0:T(128)S(1)}, s32[64]{0:T(128)}, u32[]{:S(2)}) copy-start(s32[64]{0:T(128)} %param.23) | copy-start | bytes 772
  31.2 5.5 %copy-start.4 = (s32[64]{0:T(128)S(1)}, s32[64]{0:T(128)}, u32[]{:S(2)}) copy-start(s32[64]{0:T(128)} %param.22) | copy-start | bytes 772
  76.5 56.2 %all-to-all-start = ((bf16[4,1024,576]{1,2,0:T(8,128)(2,1)}), bf16[4,1024,576]{1,2,0:T(8,128)(2,1)}, u32[]{:S(2)}, u32[]{:S(2)}) async-start(bf16[4,1024,576]{1,2,0:T(8,128)(2,1)} %copy.67), calls=%async_computation | async-start | bytes 9437184 | tf_op jit(solution)/shard_map/all_to_all | solution.py:239
  81.6 287.7 %all-gather.8.cloned.1.call-start = ((), (), s32[]{:S(2)}) async-start(), calls=%async_computation.5 | async-start | bytes 5308416 | tf_op jit(solution)/shard_map/all_gather | solution.py:271
  167.3 2.4 copy-start
  238.6 50.3 %all-to-all-start.2 = ((bf16[8,512,128]{2,1,0:T(8,128)(2,1)}), bf16[8,512,128]{2,1,0:T(8,128)(2,1)S(1)}, u32[]{:S(2)}, u32[]{:S(2)}) async-start(bf16[8,512,128]{2,1,0:T(8,128)(2,1)} %bitcast.23), calls=%async_computation.2 | async-start | bytes 2097152 | tf_op jit(solution)/shard_map/all_to_all | solution.py:256
  253.5 39.8 %copy-start.2 = (f32[31,1536]{1,0:T(8,128)S(1)}, f32[31,1536]{1,0:T(8,128)}, u32[]{:S(2)}) copy-start(f32[31,1536]{1,0:T(8,128)} %param.28) | copy-start | bytes 571396
  288.9 54.6 %all-to-all-start.1 = ((bf16[8,512,192]{1,2,0:T(8,128)(2,1)}), bf16[8,512,192]{1,2,0:T(8,128)(2,1)}, u32[]{:S(2)}, u32[]{:S(2)}) async-start(bf16[8,512,192]{1,2,0:T(8,128)(2,1)} %copy.69), calls=%async_computation.1 | async-start | bytes 3145728 | tf_op jit(solution)/shard_map/all_to_all | solution.py:258
  352.7 0.7 copy-start.6
  352.7 0.7 copy-start.7
  361.1 11.9 %copy-start.3 = (f32[1536]{0:T(1024)S(1)}, f32[1536]{0:T(1024)}, u32[]{:S(2)}) copy-start(f32[1536]{0:T(1024)} %get-tuple-element.119) | copy-start | bytes 18436
  362.0 1.2 copy-start.1
  363.2 6.1 %collective-permute-start = (bf16[15,1536]{1,0:T(8,128)(2,1)S(1)}, bf16[15,1536]{1,0:T(8,128)(2,1)}, u32[]{:S(2)}, u32[]{:S(2)}) collective-permute-start(bf16[15,1536]{1,0:T(8,128)(2,1)S(1)} %get-tuple-element.165), channel_id=1, source_target_pairs={{0,1},{1,2},{2,3},{3,4},{4,5},{5,6},{6,7},{8,9},{9,10},{10,11},{11... | collective-permute-start | bytes 138248 | tf_op jit(solution)/shard_map/ppermute | solution.py:25
  367.0 6.1 %collective-permute-start.1 = (bf16[15,1536]{1,0:T(8,128)(2,1)S(1)}, bf16[15,1536]{1,0:T(8,128)(2,1)}, u32[]{:S(2)}, u32[]{:S(2)}) collective-permute-start(bf16[15,1536]{1,0:T(8,128)(2,1)S(1)} %get-tuple-element.166), channel_id=1, source_target_pairs={{1,0},{2,1},{3,2},{4,3},{5,4},{6,5},{7,6},{9,8},{10,9},{11,10},{12... | collective-permute-start | bytes 138248 | tf_op jit(solution)/shard_map/ppermute | solution.py:27
Sparse Core Ops, SparseCore 0:
  9.5 61.2 all-gather.3
  72.8 136.4 all-gather.5
  211.5 124.2 all-gather.7
